TPU v7x, 512 devices: a whole 4x8x8 slice. The times are simulated.
512 devices in a mesh: tp: 8 (over x, y_hi), seq: 64 (over z, y_lo, core).
Axes of the slice: x: 4, y: 8 (y_hi: 2, y_lo: 4; y = y_hi * 4 + y_lo), z: 8, core: 2. Of those that a mesh axis runs over, the one named last changes fastest.
Arguments:
- llama_context: bfloat16 [512, 4096], P(None, 'tp'), may hold values from -6 to 6
- llama_residual: bfloat16 [512, 4096], P(None, 'seq'), may hold values from -6 to 6
- w_attn_out: bfloat16 [4096, 4096], P('tp', 'seq'), may hold values from -0.09375 to 0.09375
- w_caption: bfloat16 [4096, 2560], P('seq', 'tp'), may hold values from -0.09375 to 0.09375
- w_text_kv: bfloat16 [2560, 2, 2048], P(None, None, 'tp'), may hold values from -0.125 to 0.125
- prompt_length: int32 [4], replicated, may hold values from 1 to 128, as said below
- image_query: bfloat16 [2, 16384, 2048], P(None, 'seq', 'tp'), may hold values from -32 to 32
- image_key: bfloat16 [2, 16384, 2048], P(None, 'seq', 'tp'), may hold values from -9 to 9
- image_value: bfloat16 [2, 16384, 2048], P(None, 'seq', 'tp'), may hold values from -6 to 6
Outputs:
- joint_context: bfloat16 [2, 16384, 2048], P(None, 'seq', 'tp')
Inputs may be any that keep to these rules, and one draw needn't show every extreme that they name: `prompt_length`: one pair's prompt has all 128 tokens live, every other pair's fewer.
All inputs are finite; a program needn't handle non-finite values.
Results may differ from a plain program's by a relative error of at most 0.039.
Values may be sent and summed in bfloat16 or wider, within the bound.
No kernel may reach another device: no remote copies, remote signals or barrier semaphores. Data moves between devices by JAX's collectives and lax.ppermute only.
A program may use at most 64 MiB of HBM per device.

v0:
```python
import math
import jax
import jax.numpy as jnp
from jax import lax
from jax.sharding import PartitionSpec as P

TXT = 128
HD = 128
IMG = 4096


def partner(value, axis, apart):
    mask = 2**apart
    pairs = [(source, source ^ mask) for source in range(lax.axis_size(axis))]
    return lax.ppermute(value, axis, pairs)


def local(
    llama_context,
    llama_residual,
    w_attn_out,
    w_caption,
    w_text_kv,
    prompt_length,
    image_query,
    image_key,
    image_value,
):
    llama_term = jnp.dot(llama_context, w_attn_out, preferred_element_type=jnp.float32)
    llama_attn = lax.psum(llama_term.astype(jnp.bfloat16), "tp").astype(jnp.float32)
    llama_hidden = (llama_residual.astype(jnp.float32) + llama_attn).astype(jnp.bfloat16)
    seq_index = lax.axis_index("seq")
    side_count, row_count, local_width = image_query.shape
    group_size = IMG // row_count
    text_rows = TXT // group_size
    caption_term = jnp.dot(llama_hidden, w_caption, preferred_element_type=jnp.float32)
    caption_whole = lax.psum(caption_term, "seq")
    text_part = lax.dynamic_slice_in_dim(caption_whole, seq_index * text_rows, text_rows, 0)
    text_states = lax.all_gather(text_part.astype(jnp.bfloat16), "tp", axis=1, tiled=True)
    text_kv = jnp.einsum(
        "td,djc->tjc", text_states, w_text_kv, preferred_element_type=jnp.float32
    ).astype(jnp.bfloat16)
    member = seq_index % group_size
    pair_index = seq_index // group_size
    pair_count = prompt_length.shape[0]
    live_length = jnp.sum(
        jnp.where(jnp.arange(pair_count, dtype=jnp.int32) == pair_index, prompt_length, 0)
    )
    text_place = member * text_rows + jnp.arange(text_rows, dtype=jnp.int32)
    text_bias = jnp.where(text_place < live_length, 0.0, -1e30).astype(jnp.bfloat16)
    local_heads = local_width // HD
    scale_factor = 1.0 / math.sqrt(HD)
    queries = image_query.reshape(side_count, row_count, local_heads, HD)

    def absorb(running, pieces):
        old_max, old_totals, old_accum = running
        text_piece, bias_piece, key_piece, value_piece = pieces
        text_count = text_piece.shape[0]
        piece_rows = key_piece.shape[1]
        text_keys = text_piece[:, 0].reshape(text_count, local_heads, HD)
        text_values = text_piece[:, 1].reshape(text_count, local_heads, HD)
        key_heads = key_piece.reshape(side_count, piece_rows, local_heads, HD)
        value_heads = value_piece.reshape(side_count, piece_rows, local_heads, HD)
        text_scores = (
            jnp.einsum("srhd,thd->shrt", queries, text_keys, preferred_element_type=jnp.float32)
            * scale_factor
        )
        text_scores = text_scores + bias_piece.astype(jnp.float32)[None, None, None, :]
        image_scores = (
            jnp.einsum("srhd,snhd->shrn", queries, key_heads, preferred_element_type=jnp.float32)
            * scale_factor
        )
        new_max = jnp.maximum(
            old_max, jnp.maximum(jnp.max(text_scores, axis=-1), jnp.max(image_scores, axis=-1))
        )
        factor = jnp.exp(old_max - new_max)
        text_weights = jnp.exp(text_scores - new_max[..., None])
        image_weights = jnp.exp(image_scores - new_max[..., None])
        new_totals = (
            old_totals * factor + jnp.sum(text_weights, axis=-1) + jnp.sum(image_weights, axis=-1)
        )
        addition = jnp.einsum(
            "shrt,thd->shrd",
            text_weights.astype(jnp.bfloat16),
            text_values,
            preferred_element_type=jnp.float32,
        )
        addition = addition + jnp.einsum(
            "shrn,snhd->shrd",
            image_weights.astype(jnp.bfloat16),
            value_heads,
            preferred_element_type=jnp.float32,
        )
        return (new_max, new_totals, old_accum * factor[..., None] + addition)

    start_max = jnp.full((side_count, local_heads, row_count), -1e30, jnp.float32)
    start_totals = jnp.zeros((side_count, local_heads, row_count), jnp.float32)
    start_accum = jnp.zeros((side_count, local_heads, row_count, HD), jnp.float32)
    collected = (text_kv, text_bias, image_key, image_value)
    running = absorb((start_max, start_totals, start_accum), collected)
    levels = group_size.bit_length() - 1
    bit_order = list(range(levels))
    for position, bit_number in enumerate(bit_order):
        arrived = partner(
            (collected[0], collected[1], collected[2], collected[3]), "seq", bit_number
        )
        running = absorb(running, arrived)
        if position + 1 < levels:
            collected = (
                jnp.concatenate((collected[0], arrived[0]), axis=0),
                jnp.concatenate((collected[1], arrived[1]), axis=0),
                jnp.concatenate((collected[2], arrived[2]), axis=1),
                jnp.concatenate((collected[3], arrived[3]), axis=1),
            )
    final_max, final_totals, final_accum = running
    context = (final_accum / final_totals[..., None]).astype(jnp.bfloat16)
    return context.transpose(0, 2, 1, 3).reshape(side_count, row_count, local_width)


def solution(mesh):
    placed = (
        P(None, "tp"),
        P(None, "seq"),
        P("tp", "seq"),
        P("seq", "tp"),
        P(None, None, "tp"),
        P(),
        P(None, "seq", "tp"),
        P(None, "seq", "tp"),
        P(None, "seq", "tp"),
    )
    return jax.shard_map(
        local, mesh=mesh, in_specs=placed, out_specs=P(None, "seq", "tp"), check_vma=False
    )
```

profile of v0, /device:TPU:1, one launch (start us, length us, event | category | flops | bytes accessed | tf_op | source)
XLA Modules:
  0.0 641.8 jit_solution(18367367319555831022)
XLA Ops:
  6.6 1.4 fusion.127
  8.0 1.2 fusion.139
  9.2 8.7 %collective-permute-start.1 = (bf16[8]{0:T(256)(128)(2,1)S(1)}, bf16[8]{0:T(256)(128)(2,1)S(1)}, u32[]{:S(2)}, u32[]{:S(2)}) collective-permute-start(bf16[8]{0:T(256)(128)(2,1)S(1)} %get-tuple-element.18), channel_id=1, source_target_pairs={{0,1},{1,0},{2,3},{3,2},{4,5},{5,4},{6,7},{7,6},{8,9},{9,8},{10,11... | collective-permute-start | bytes 56 | tf_op jit(solution)/shard_map/ppermute | solution.py:15
  17.9 2.0 convolution_convert_fusion
  19.9 1.1 copy.207
  21.0 1.9 collective-permute-start.2
  22.9 1.8 copy.212
  24.7 2.4 collective-permute-start.3
  27.1 2.9 fusion.150
  30.1 1.9 collective-permute-start.5
  32.0 2.4 collective-permute-done.5
  34.5 1.9 collective-permute-start.9
  36.9 2.7 collective-permute-done.9
  39.7 1.9 collective-permute-start.13
  42.8 1.3 collective-permute-done.13
  44.6 79.9 %all-reduce.3.cloned.1.call-done = bf16[512,64]{0,1:T(8,128)(2,1)} async-done(((bf16[512,64]{0,1:T(8,128)(2,1)}), bf16[512,64]{0,1:T(8,128)(2,1)}) %all-reduce.3.cloned.1.call-update) | async-done | bytes 65552 | tf_op jit(solution)/shard_map/psum | solution.py:30
  124.6 2.0 fusion.97
  126.6 272.4 %all-reduce.4 = bf16[512,320]{1,0:T(8,128)(2,1)} all-reduce(f32[512,320]{1,0:T(8,128)} %fusion.97), channel_id=1, replica_groups=mesh['tp'=8,'seq'=64] {'seq'}, use_global_device_ids=true, to_apply=%region_1.0 | all-reduce | flops 163840 | bytes 983040 | tf_op jit(solution)/shard_map/psum | solution.py:37
  398.9 0.7 fusion.117
  399.6 37.7 %all-gather = bf16[8,320,8]{1,2,0:T(8,128)(2,1)S(1)} all-gather(bf16[1,320,8]{1,2,0:T(8,128)(2,1)S(1)} %fusion.117), channel_id=1, replica_groups=mesh['tp'=8,'seq'=64] {'tp'}, dimensions={0}, use_global_device_ids=true | all-gather | bytes 46080 | tf_op jit(solution)/shard_map/all_gather | solution.py:39
  437.9 14.5 %collective-permute-start = (bf16[8,2,256]{2,0,1:T(8,128)(2,1)S(1)}, bf16[8,2,256]{2,0,1:T(8,128)(2,1)S(1)}, u32[]{:S(2)}, u32[]{:S(2)}) collective-permute-start(bf16[8,2,256]{2,0,1:T(8,128)(2,1)S(1)} %fusion.50), channel_id=1, source_target_pairs={{0,1},{1,0},{2,3},{3,2},{4,5},{5,4},{6,7},{7,6},{8,9},{9,8},{10,11... | collective-permute-start | bytes 24584 | tf_op jit(solution)/shard_map/ppermute | solution.py:15
  452.4 0.8 fusion.149
  453.2 1.9 collective-permute-start.4
  455.2 0.7 copy-done.4
  455.9 0.8 pad_maximum_fusion.4
  456.7 3.3 collective-permute-start.6
  460.1 0.8 fusion.147
  460.9 0.6 pad_maximum_fusion.7
  461.5 1.9 collective-permute-start.8
  464.0 0.6 reshape_squeeze.34
  464.6 8.0 %collective-permute-done.6 = bf16[2,512,256]{1,2,0:T(8,128)(2,1)S(1)} collective-permute-done((bf16[2,512,256]{1,2,0:T(8,128)(2,1)}, bf16[2,512,256]{1,2,0:T(8,128)(2,1)S(1)}, u32[]{:S(2)}, u32[]{:S(2)}) %collective-permute-start.6) | collective-permute-done | bytes 524320 | tf_op jit(solution)/shard_map/ppermute | solution.py:15
  472.6 2.2 pad_maximum_fusion.2
  474.8 1.9 collective-permute-start.10
  476.7 1.4 fusion.146
  478.2 1.3 reshape_squeeze.35
  479.5 1.4 pad_maximum_fusion.6
  480.9 1.9 collective-permute-start.12
  482.8 1.3 fusion.142
  484.1 1.3 reshape_squeeze.36
  485.4 1.3 reshape_squeeze.37
  486.8 2.2 fusion.145
  488.9 1.9 pad_maximum_fusion.5
  490.8 2.4 collective-permute-start.7
  493.2 1.4 fusion.141
  494.6 1.4 reshape_squeeze.38
  496.0 29.3 %collective-permute-done.10 = bf16[2,1024,256]{1,2,0:T(8,128)(2,1)} collective-permute-done((bf16[2,1024,256]{1,2,0:T(8,128)(2,1)}, bf16[2,1024,256]{1,2,0:T(8,128)(2,1)}, u32[]{:S(2)}, u32[]{:S(2)}) %collective-permute-start.10) | collective-permute-done | bytes 1048608 | tf_op jit(solution)/shard_map/ppermute | solution.py:15
  525.3 3.0 pad_maximum_fusion
  528.3 1.9 collective-permute-start.14
  530.2 1.5 fusion.144
  531.7 1.4 reshape_squeeze.39
  533.1 1.3 pad_maximum_fusion.3
  534.5 1.9 collective-permute-start.11
  538.1 44.0 %collective-permute-done.11 = bf16[2,1024,256]{1,2,0:T(8,128)(2,1)S(1)} collective-permute-done((bf16[2,1024,256]{1,2,0:T(8,128)(2,1)S(1)}, bf16[2,1024,256]{1,2,0:T(8,128)(2,1)S(1)}, u32[]{:S(2)}, u32[]{:S(2)}) %collective-permute-start.11) | collective-permute-done | bytes 1048608 | tf_op jit(solution)/shard_map/ppermute | solution.py:15
  582.1 1.4 pad_maximum_fusion.1
  583.5 3.5 collective-permute-start.15
  587.1 2.0 bitcast_reduce_fusion.1
  589.1 3.0 bitcast_reduce_fusion
  592.8 1.3 convolution_bitcast_fusion.4
  594.6 1.2 convolution_bitcast_fusion.5
  595.8 0.8 fusion.7
  597.0 1.6 fusion.1
  598.7 33.4 %collective-permute-done.15 = bf16[2,2048,256]{1,2,0:T(8,128)(2,1)S(1)} collective-permute-done((bf16[2,2048,256]{1,2,0:T(8,128)(2,1)S(1)}, bf16[2,2048,256]{1,2,0:T(8,128)(2,1)S(1)}, u32[]{:S(2)}, u32[]{:S(2)}) %collective-permute-start.15) | collective-permute-done | bytes 2097184 | tf_op jit(solution)/shard_map/ppermute | solution.py:15
  632.1 0.7 fusion.23
  634.1 0.8 copy.254
  (99 shorter events, 8.1 us)
Async XLA Ops:
  6.5 430.9 %copy-start = (bf16[2560,2,256]{2,1,0:T(2,128)(2,1)S(1)}, bf16[2560,2,256]{2,1,0:T(2,128)(2,1)}, u32[]{:S(2)}) copy-start(bf16[2560,2,256]{2,1,0:T(2,128)(2,1)} %param.13) | copy-start | bytes 7864324
  6.5 118.0 %copy-start.12 = (bf16[512,64]{0,1:T(8,128)(2,1)S(1)}, bf16[512,64]{0,1:T(8,128)(2,1)}, u32[]{:S(2)}) copy-start(bf16[512,64]{0,1:T(8,128)(2,1)} %param.10) | copy-start | bytes 196612
  6.5 118.0 %copy-start.13 = (bf16[64,320]{1,0:T(8,128)(2,1)S(1)}, bf16[64,320]{1,0:T(8,128)(2,1)}, u32[]{:S(2)}) copy-start(bf16[64,320]{1,0:T(8,128)(2,1)} %param.12) | copy-start | bytes 122884
  6.5 118.0 %all-reduce.3.cloned.1.call-start = ((), (), s32[]{:S(2)}) async-start(), calls=%async_computation | async-start | bytes 131072 | tf_op jit(solution)/shard_map/psum | solution.py:30
  9.2 20.8 %collective-permute-start.1 = (bf16[8]{0:T(256)(128)(2,1)S(1)}, bf16[8]{0:T(256)(128)(2,1)S(1)}, u32[]{:S(2)}, u32[]{:S(2)}) collective-permute-start(bf16[8]{0:T(256)(128)(2,1)S(1)} %get-tuple-element.18), channel_id=1, source_target_pairs={{0,1},{1,0},{2,3},{3,2},{4,5},{5,4},{6,7},{7,6},{8,9},{9,8},{10,11... | collective-permute-start | bytes 56 | tf_op jit(solution)/shard_map/ppermute | solution.py:15
  21.0 434.2 %copy-start.3 = (bf16[2,256,256]{1,2,0:T(8,128)(2,1)}, bf16[2,256,256]{1,2,0:T(8,128)(2,1)S(1)}, u32[]{:S(2)}) copy-start(bf16[2,256,256]{1,2,0:T(8,128)(2,1)S(1)} %copy.207) | copy-start | bytes 786436
  21.0 434.2 %collective-permute-start.2 = (bf16[2,256,256]{1,2,0:T(8,128)(2,1)S(1)}, bf16[2,256,256]{1,2,0:T(8,128)(2,1)S(1)}, u32[]{:S(2)}, u32[]{:S(2)}) collective-permute-start(bf16[2,256,256]{1,2,0:T(8,128)(2,1)S(1)} %copy.207), channel_id=1, source_target_pairs={{0,1},{1,0},{2,3},{3,2},{4,5},{5,4},{6,7},{7,6},{8,9},{9,8},{10,11... | collective-permute-start | bytes 786440 | tf_op jit(solution)/shard_map/ppermute | solution.py:15
  24.7 464.2 %collective-permute-start.3 = (bf16[2,256,256]{1,2,0:T(8,128)(2,1)}, bf16[2,256,256]{1,2,0:T(8,128)(2,1)}, u32[]{:S(2)}, u32[]{:S(2)}) collective-permute-start(bf16[2,256,256]{1,2,0:T(8,128)(2,1)} %copy.212), channel_id=1, source_target_pairs={{0,1},{1,0},{2,3},{3,2},{4,5},{5,4},{6,7},{7,6},{8,9},{9,8},{10,11... | collective-permute-start | bytes 786440 | tf_op jit(solution)/shard_map/ppermute | solution.py:15
  30.1 4.3 collective-permute-start.5
  34.5 5.2 collective-permute-start.9
  39.7 4.3 collective-permute-start.13
  126.6 325.9 %copy-start.1 = (bf16[2,256,256]{2,1,0:T(8,128)(2,1)S(1)}, bf16[2,256,256]{2,1,0:T(8,128)(2,1)}, u32[]{:S(2)}) copy-start(bf16[2,256,256]{2,1,0:T(8,128)(2,1)} %param.15) | copy-start | bytes 786436
  126.6 325.9 %copy-start.23 = (f32[8]{0:T(128)S(1)}, f32[8]{0:T(128)}, u32[]{:S(2)}) copy-start(f32[8]{0:T(128)} %get-tuple-element.17) | copy-start | bytes 100
  437.4 22.7 %copy-start.25 = (f32[8]{0:T(128)S(1)}, f32[8]{0:T(128)}, u32[]{:S(2)}) copy-start(f32[8]{0:T(128)} %convert_element_type.88) | copy-start | bytes 100
  437.9 15.3 %collective-permute-start = (bf16[8,2,256]{2,0,1:T(8,128)(2,1)S(1)}, bf16[8,2,256]{2,0,1:T(8,128)(2,1)S(1)}, u32[]{:S(2)}, u32[]{:S(2)}) collective-permute-start(bf16[8,2,256]{2,0,1:T(8,128)(2,1)S(1)} %fusion.50), channel_id=1, source_target_pairs={{0,1},{1,0},{2,3},{3,2},{4,5},{5,4},{6,7},{7,6},{8,9},{9,8},{10,11... | collective-permute-start | bytes 24584 | tf_op jit(solution)/shard_map/ppermute | solution.py:15
  453.2 7.6 %collective-permute-start.4 = (bf16[16,2,256]{2,0,1:T(8,128)(2,1)S(1)}, bf16[16,2,256]{2,0,1:T(8,128)(2,1)S(1)}, u32[]{:S(2)}, u32[]{:S(2)}) collective-permute-start(bf16[16,2,256]{2,0,1:T(8,128)(2,1)S(1)} %pad_maximum_fusion.8), channel_id=1, source_target_pairs={{0,2},{1,3},{2,0},{3,1},{4,6},{5,7},{6,4},{7,5},{8,10},{9,11},{10,... | collective-permute-start | bytes 49160 | tf_op jit(solution)/shard_map/ppermute | solution.py:15
  455.2 0.7 copy-start.4
  456.7 15.9 %collective-permute-start.6 = (bf16[2,512,256]{1,2,0:T(8,128)(2,1)}, bf16[2,512,256]{1,2,0:T(8,128)(2,1)S(1)}, u32[]{:S(2)}, u32[]{:S(2)}) collective-permute-start(bf16[2,512,256]{1,2,0:T(8,128)(2,1)} %pad_maximum_fusion.4), channel_id=1, source_target_pairs={{0,2},{1,3},{2,0},{3,1},{4,6},{5,7},{6,4},{7,5},{8,10},{9,11},{10,... | collective-permute-start | bytes 1572872 | tf_op jit(solution)/shard_map/ppermute | solution.py:15
  460.9 2.5 copy-start.9
  461.5 18.0 %collective-permute-start.8 = (bf16[32,2,256]{2,0,1:T(8,128)(2,1)}, bf16[32,2,256]{2,0,1:T(8,128)(2,1)}, u32[]{:S(2)}, u32[]{:S(2)}) collective-permute-start(bf16[32,2,256]{2,0,1:T(8,128)(2,1)} %pad_maximum_fusion.7), channel_id=1, source_target_pairs={{0,4},{1,5},{2,6},{3,7},{4,0},{5,1},{6,2},{7,3},{8,12},{9,13},{10,... | collective-permute-start | bytes 98312 | tf_op jit(solution)/shard_map/ppermute | solution.py:15
  464.6 12.1 %copy-start.19 = (bf16[16,2,128]{2,1,0:T(2,128)(2,1)S(1)}, bf16[16,2,128]{2,1,0:T(2,128)(2,1)}, u32[]{:S(2)}) copy-start(bf16[16,2,128]{2,1,0:T(2,128)(2,1)} %reshape_squeeze.34) | copy-start | bytes 24580
  474.8 50.5 %collective-permute-start.10 = (bf16[2,1024,256]{1,2,0:T(8,128)(2,1)}, bf16[2,1024,256]{1,2,0:T(8,128)(2,1)}, u32[]{:S(2)}, u32[]{:S(2)}) collective-permute-start(bf16[2,1024,256]{1,2,0:T(8,128)(2,1)} %pad_maximum_fusion.2), channel_id=1, source_target_pairs={{0,4},{1,5},{2,6},{3,7},{4,0},{5,1},{6,2},{7,3},{8,12},{9,13},{10,... | collective-permute-start | bytes 3145736 | tf_op jit(solution)/shard_map/ppermute | solution.py:15
  480.9 12.3 %collective-permute-start.12 = (bf16[64,2,256]{2,0,1:T(8,128)(2,1)}, bf16[64,2,256]{2,0,1:T(8,128)(2,1)}, u32[]{:S(2)}, u32[]{:S(2)}) collective-permute-start(bf16[64,2,256]{2,0,1:T(8,128)(2,1)} %pad_maximum_fusion.6), channel_id=1, source_target_pairs={{0,8},{1,9},{2,10},{3,11},{4,12},{5,13},{6,14},{7,15},{8,0},{9,1},... | collective-permute-start | bytes 196616 | tf_op jit(solution)/shard_map/ppermute | solution.py:15
  490.8 42.3 %collective-permute-start.7 = (bf16[2,512,256]{1,2,0:T(8,128)(2,1)}, bf16[2,512,256]{1,2,0:T(8,128)(2,1)}, u32[]{:S(2)}, u32[]{:S(2)}) collective-permute-start(bf16[2,512,256]{1,2,0:T(8,128)(2,1)} %pad_maximum_fusion.5), channel_id=1, source_target_pairs={{0,2},{1,3},{2,0},{3,1},{4,6},{5,7},{6,4},{7,5},{8,10},{9,11},{10,... | collective-permute-start | bytes 1572872 | tf_op jit(solution)/shard_map/ppermute | solution.py:15
  496.0 34.2 %copy-start.10 = (bf16[64,2,128]{2,1,0:T(2,128)(2,1)S(1)}, bf16[64,2,128]{2,1,0:T(2,128)(2,1)}, u32[]{:S(2)}) copy-start(bf16[64,2,128]{2,1,0:T(2,128)(2,1)} %reshape_squeeze.38) | copy-start | bytes 98308
  496.0 34.2 %copy-start.24 = (f32[64]{0:T(128)S(1)}, f32[64]{0:T(128)}, u32[]{:S(2)}) copy-start(f32[64]{0:T(128)} %convert_element_type.97) | copy-start | bytes 772
  528.3 60.8 %collective-permute-start.14 = (bf16[2,2048,256]{1,2,0:T(8,128)(2,1)}, bf16[2,2048,256]{1,2,0:T(8,128)(2,1)}, u32[]{:S(2)}, u32[]{:S(2)}) collective-permute-start(bf16[2,2048,256]{1,2,0:T(8,128)(2,1)} %pad_maximum_fusion), channel_id=1, source_target_pairs={{0,8},{1,9},{2,10},{3,11},{4,12},{5,13},{6,14},{7,15},{8,0},{9,1},... | collective-permute-start | bytes 6291464 | tf_op jit(solution)/shard_map/ppermute | solution.py:15
  533.1 3.3 copy-start.5
  534.5 47.7 %collective-permute-start.11 = (bf16[2,1024,256]{1,2,0:T(8,128)(2,1)S(1)}, bf16[2,1024,256]{1,2,0:T(8,128)(2,1)S(1)}, u32[]{:S(2)}, u32[]{:S(2)}) collective-permute-start(bf16[2,1024,256]{1,2,0:T(8,128)(2,1)S(1)} %pad_maximum_fusion.3), channel_id=1, source_target_pairs={{0,4},{1,5},{2,6},{3,7},{4,0},{5,1},{6,2},{7,3},{8,12},{9,13},{10,... | collective-permute-start | bytes 3145736 | tf_op jit(solution)/shard_map/ppermute | solution.py:15
  536.4 0.9 copy-start.15
  536.4 0.9 copy-start.17
  536.4 0.9 copy-start.20
  536.4 0.9 copy-start.21
  536.4 1.2 copy-start.2
  536.8 1.0 copy-start.7
  583.5 48.6 %collective-permute-start.15 = (bf16[2,2048,256]{1,2,0:T(8,128)(2,1)S(1)}, bf16[2,2048,256]{1,2,0:T(8,128)(2,1)S(1)}, u32[]{:S(2)}, u32[]{:S(2)}) collective-permute-start(bf16[2,2048,256]{1,2,0:T(8,128)(2,1)S(1)} %pad_maximum_fusion.1), channel_id=1, source_target_pairs={{0,8},{1,9},{2,10},{3,11},{4,12},{5,13},{6,14},{7,15},{8,0},{9,1},... | collective-permute-start | bytes 6291464 | tf_op jit(solution)/shard_map/ppermute | solution.py:15
  589.1 3.0 copy-start.14
  589.1 3.0 copy-start.16
  589.1 3.0 copy-start.6
  589.1 3.1 copy-start.8
  592.3 1.8 copy-start.18
  632.1 0.8 copy-start.11
  632.9 0.9 copy-start.22
Sparse Core Ops, SparseCore 0:
  20.0 104.4 all-reduce.2
where the time goes:
time: 644 us; the launch traced here: 642 us
  blocking collectives  310 us (48%)
  waiting for transfers between devices  201 us (31%)
  starting transfers between devices  54 us (8%)
  matrix products  25.1 us (4%)
  other arithmetic  21.1 us (3%)
  local copies, waits for them, and re-layouts  16.3 us (3%)
  between operations  14.1 us (2%)
    psum x1, blocking collectives, local(): caption_whole = lax.psum(caption_term, 'seq')  272 us
    ppermute x16, waiting for transfers between devices, partner(): return lax.ppermute(value, axis, pairs)  121 us
    psum x1, waiting for transfers between devices, local(): lax.psum(llama_term.astype(jnp.bfloat16), 'tp').astype(jnp.float32)  79.9 us
    ppermute x16, starting transfers between devices, partner(): return lax.ppermute(value, axis, pairs)  54 us
    all_gather x1, blocking collectives, local(): lax.all_gather(text_part.astype(jnp.bfloat16), 'tp', axis=1, tiled=True)  37.7 us
  transfers between devices with their start and end apart: 17, of which 8 were waited for; matrix products, arithmetic and copies ran while one was open for 9% of the time, Pallas kernels for 0%

commit v1 on v0

--- a/solution.py
+++ b/solution.py
@@ -36,7 +36,12 @@
     caption_term = jnp.dot(llama_hidden, w_caption, preferred_element_type=jnp.float32)
     caption_whole = lax.psum(caption_term, "seq")
     text_part = lax.dynamic_slice_in_dim(caption_whole, seq_index * text_rows, text_rows, 0)
-    text_states = lax.all_gather(text_part.astype(jnp.bfloat16), "tp", axis=1, tiled=True)
+    text_states = jnp.concatenate(
+        lax.all_to_all(
+            jnp.stack([text_part.astype(jnp.bfloat16)] * lax.axis_size("tp")), "tp", 0, 0
+        ),
+        axis=1,
+    )
     text_kv = jnp.einsum(
         "td,djc->tjc", text_states, w_text_kv, preferred_element_type=jnp.float32
     ).astype(jnp.bfloat16)

time: 644 us -> 615 us (0.955)
  blocking collectives: 310 us -> 272 us
  waiting for transfers between devices: 201 us -> 211 us
    all_gather x1 -> x0, blocking collectives: 37.7 us -> none  [local(): lax.all_gather(text_part.astype(jnp.bfloat16), 'tp', axis=1, tiled=True)]
    psum x1, waiting for transfers between devices: 79.9 us -> 88.2 us  [local(): lax.psum(llama_term.astype(jnp.bfloat16), 'tp').astype(jnp.float32)]
  transfers between devices with their start and end apart: 17 -> 18, of which waited for: 8 -> 8; matrix products, arithmetic and copies ran while one was open for 9% -> 9% of each run, Pallas kernels for 0% -> 0%
where the time goes in v1:
time: 615 us; the launch traced here: 613 us
  blocking collectives  272 us (44%)
  waiting for transfers between devices  211 us (34%)
  starting transfers between devices  52.3 us (9%)
  matrix products  25.7 us (4%)
  other arithmetic  21.1 us (3%)
  local copies, waits for them, and re-layouts  17 us (3%)
  between operations  14.1 us (2%)
    psum x1, blocking collectives, local(): caption_whole = lax.psum(caption_term, 'seq')  272 us
    ppermute x16, waiting for transfers between devices, partner(): return lax.ppermute(value, axis, pairs)  118 us
    psum x1, waiting for transfers between devices, local(): lax.psum(llama_term.astype(jnp.bfloat16), 'tp').astype(jnp.float32)  88.2 us
    ppermute x16, starting transfers between devices, partner(): return lax.ppermute(value, axis, pairs)  49 us
  transfers between devices with their start and end apart: 18, of which 8 were waited for; matrix products, arithmetic and copies ran while one was open for 9% of the time, Pallas kernels for 0%

profile of v1, /device:TPU:1, one launch (start us, length us, event | category | flops | bytes accessed | tf_op | source)
XLA Modules:
  0.0 613.1 jit_solution(5446837464490521098)
XLA Ops:
  6.6 1.4 fusion.126
  8.0 1.2 fusion.138
  9.2 8.7 %collective-permute-start.1 = (bf16[8]{0:T(256)(128)(2,1)S(1)}, bf16[8]{0:T(256)(128)(2,1)S(1)}, u32[]{:S(2)}, u32[]{:S(2)}) collective-permute-start(bf16[8]{0:T(256)(128)(2,1)S(1)} %get-tuple-element.18), channel_id=1, source_target_pairs={{0,1},{1,0},{2,3},{3,2},{4,5},{5,4},{6,7},{7,6},{8,9},{9,8},{10,11... | collective-permute-start | bytes 56 | tf_op jit(solution)/shard_map/ppermute | solution.py:15
  17.9 2.0 convolution_convert_fusion
  19.9 1.1 copy.206
  21.0 1.9 collective-permute-start.2
  23.0 1.8 copy.211
  24.7 2.4 collective-permute-start.3
  27.1 2.9 fusion.149
  30.1 1.9 collective-permute-start.5
  32.6 1.8 collective-permute-done.5
  34.5 1.9 collective-permute-start.9
  36.4 88.2 %all-reduce.3.cloned.1.call-done = bf16[512,64]{0,1:T(8,128)(2,1)} async-done(((bf16[512,64]{0,1:T(8,128)(2,1)}), bf16[512,64]{0,1:T(8,128)(2,1)}) %all-reduce.3.cloned.1.call-update) | async-done | bytes 65552 | tf_op jit(solution)/shard_map/psum | solution.py:30
  124.6 2.0 fusion.97
  126.6 272.4 %all-reduce.4 = bf16[512,320]{1,0:T(8,128)(2,1)} all-reduce(f32[512,320]{1,0:T(8,128)} %fusion.97), channel_id=1, replica_groups=mesh['tp'=8,'seq'=64] {'seq'}, use_global_device_ids=true, to_apply=%region_1.0 | all-reduce | flops 163840 | bytes 983040 | tf_op jit(solution)/shard_map/psum | solution.py:37
  399.0 0.7 dynamic-slice_convert_fusion
  399.7 0.6 stack.2
  400.3 3.3 all-to-all-start
  403.8 1.9 collective-permute-start.13
  406.7 1.3 collective-permute-done.13
  408.6 4.1 all-to-all-done
  413.2 9.5 %collective-permute-start = (bf16[8,2,256]{2,0,1:T(8,128)(2,1)S(1)}, bf16[8,2,256]{2,0,1:T(8,128)(2,1)S(1)}, u32[]{:S(2)}, u32[]{:S(2)}) collective-permute-start(bf16[8,2,256]{2,0,1:T(8,128)(2,1)S(1)} %fusion.50), channel_id=1, source_target_pairs={{0,1},{1,0},{2,3},{3,2},{4,5},{5,4},{6,7},{7,6},{8,9},{9,8},{10,11... | collective-permute-start | bytes 24584 | tf_op jit(solution)/shard_map/ppermute | solution.py:15
  422.7 1.4 fusion.148
  424.1 1.9 collective-permute-start.4
  426.1 0.7 copy-done.4
  426.8 0.8 pad_maximum_fusion.4
  427.6 3.3 collective-permute-start.6
  431.0 0.8 fusion.146
  431.8 0.6 pad_maximum_fusion.7
  432.4 1.9 collective-permute-start.8
  435.5 8.3 %collective-permute-done.6 = bf16[2,512,256]{1,2,0:T(8,128)(2,1)S(1)} collective-permute-done((bf16[2,512,256]{1,2,0:T(8,128)(2,1)}, bf16[2,512,256]{1,2,0:T(8,128)(2,1)S(1)}, u32[]{:S(2)}, u32[]{:S(2)}) %collective-permute-start.6) | collective-permute-done | bytes 524320 | tf_op jit(solution)/shard_map/ppermute | solution.py:15
  443.9 2.2 pad_maximum_fusion.2
  446.0 1.9 collective-permute-start.10
  448.0 1.4 fusion.145
  449.4 1.3 reshape_squeeze.35
  450.7 1.4 pad_maximum_fusion.6
  452.1 1.9 collective-permute-start.12
  454.0 1.4 fusion.141
  455.3 1.3 reshape_squeeze.36
  456.7 1.3 reshape_squeeze.37
  458.0 2.2 fusion.144
  460.2 1.9 pad_maximum_fusion.5
  462.0 2.4 collective-permute-start.7
  464.4 1.4 fusion.140
  465.8 1.4 reshape_squeeze.38
  467.2 29.3 %collective-permute-done.10 = bf16[2,1024,256]{1,2,0:T(8,128)(2,1)} collective-permute-done((bf16[2,1024,256]{1,2,0:T(8,128)(2,1)}, bf16[2,1024,256]{1,2,0:T(8,128)(2,1)}, u32[]{:S(2)}, u32[]{:S(2)}) %collective-permute-start.10) | collective-permute-done | bytes 1048608 | tf_op jit(solution)/shard_map/ppermute | solution.py:15
  496.6 3.0 pad_maximum_fusion
  499.5 1.9 collective-permute-start.14
  501.5 1.5 fusion.143
  503.0 1.4 reshape_squeeze.39
  504.4 1.3 pad_maximum_fusion.3
  505.7 1.9 collective-permute-start.11
  509.4 44.0 %collective-permute-done.11 = bf16[2,1024,256]{1,2,0:T(8,128)(2,1)S(1)} collective-permute-done((bf16[2,1024,256]{1,2,0:T(8,128)(2,1)S(1)}, bf16[2,1024,256]{1,2,0:T(8,128)(2,1)S(1)}, u32[]{:S(2)}, u32[]{:S(2)}) %collective-permute-start.11) | collective-permute-done | bytes 1048608 | tf_op jit(solution)/shard_map/ppermute | solution.py:15
  553.4 1.4 pad_maximum_fusion.1
  554.8 3.5 collective-permute-start.15
  558.3 2.0 bitcast_reduce_fusion.1
  560.4 3.0 bitcast_reduce_fusion
  564.0 1.3 convolution_bitcast_fusion.4
  565.9 1.2 convolution_bitcast_fusion.5
  567.0 0.8 fusion.7
  568.3 1.6 fusion.1
  569.9 33.4 %collective-permute-done.15 = bf16[2,2048,256]{1,2,0:T(8,128)(2,1)S(1)} collective-permute-done((bf16[2,2048,256]{1,2,0:T(8,128)(2,1)S(1)}, bf16[2,2048,256]{1,2,0:T(8,128)(2,1)S(1)}, u32[]{:S(2)}, u32[]{:S(2)}) %collective-permute-start.15) | collective-permute-done | bytes 2097184 | tf_op jit(solution)/shard_map/ppermute | solution.py:15
  603.4 0.7 fusion.23
  605.4 0.8 copy.253
  (99 shorter events, 8.7 us)
Async XLA Ops:
  6.5 406.2 %copy-start = (bf16[2560,2,256]{2,1,0:T(2,128)(2,1)S(1)}, bf16[2560,2,256]{2,1,0:T(2,128)(2,1)}, u32[]{:S(2)}) copy-start(bf16[2560,2,256]{2,1,0:T(2,128)(2,1)} %param.13) | copy-start | bytes 7864324
  6.5 118.1 %copy-start.12 = (bf16[512,64]{0,1:T(8,128)(2,1)S(1)}, bf16[512,64]{0,1:T(8,128)(2,1)}, u32[]{:S(2)}) copy-start(bf16[512,64]{0,1:T(8,128)(2,1)} %param.10) | copy-start | bytes 196612
  6.5 118.1 %copy-start.13 = (bf16[64,320]{1,0:T(8,128)(2,1)S(1)}, bf16[64,320]{1,0:T(8,128)(2,1)}, u32[]{:S(2)}) copy-start(bf16[64,320]{1,0:T(8,128)(2,1)} %param.12) | copy-start | bytes 122884
  6.5 118.1 %all-reduce.3.cloned.1.call-start = ((), (), s32[]{:S(2)}) async-start(), calls=%async_computation.1 | async-start | bytes 131072 | tf_op jit(solution)/shard_map/psum | solution.py:30
  9.2 20.8 %collective-permute-start.1 = (bf16[8]{0:T(256)(128)(2,1)S(1)}, bf16[8]{0:T(256)(128)(2,1)S(1)}, u32[]{:S(2)}, u32[]{:S(2)}) collective-permute-start(bf16[8]{0:T(256)(128)(2,1)S(1)} %get-tuple-element.18), channel_id=1, source_target_pairs={{0,1},{1,0},{2,3},{3,2},{4,5},{5,4},{6,7},{7,6},{8,9},{9,8},{10,11... | collective-permute-start | bytes 56 | tf_op jit(solution)/shard_map/ppermute | solution.py:15
  21.0 405.1 %copy-start.3 = (bf16[2,256,256]{1,2,0:T(8,128)(2,1)}, bf16[2,256,256]{1,2,0:T(8,128)(2,1)S(1)}, u32[]{:S(2)}) copy-start(bf16[2,256,256]{1,2,0:T(8,128)(2,1)S(1)} %copy.206) | copy-start | bytes 786436
  21.0 405.0 %collective-permute-start.2 = (bf16[2,256,256]{1,2,0:T(8,128)(2,1)S(1)}, bf16[2,256,256]{1,2,0:T(8,128)(2,1)S(1)}, u32[]{:S(2)}, u32[]{:S(2)}) collective-permute-start(bf16[2,256,256]{1,2,0:T(8,128)(2,1)S(1)} %copy.206), channel_id=1, source_target_pairs={{0,1},{1,0},{2,3},{3,2},{4,5},{5,4},{6,7},{7,6},{8,9},{9,8},{10,11... | collective-permute-start | bytes 786440 | tf_op jit(solution)/shard_map/ppermute | solution.py:15
  24.7 435.4 %collective-permute-start.3 = (bf16[2,256,256]{1,2,0:T(8,128)(2,1)}, bf16[2,256,256]{1,2,0:T(8,128)(2,1)}, u32[]{:S(2)}, u32[]{:S(2)}) collective-permute-start(bf16[2,256,256]{1,2,0:T(8,128)(2,1)} %copy.211), channel_id=1, source_target_pairs={{0,1},{1,0},{2,3},{3,2},{4,5},{5,4},{6,7},{7,6},{8,9},{9,8},{10,11... | collective-permute-start | bytes 786440 | tf_op jit(solution)/shard_map/ppermute | solution.py:15
  30.1 4.3 collective-permute-start.5
  34.5 369.2 %collective-permute-start.9 = (bf16[32]{0:T(256)(128)(2,1)S(1)}, bf16[32]{0:T(256)(128)(2,1)S(1)}, u32[]{:S(2)}, u32[]{:S(2)}) collective-permute-start(bf16[32]{0:T(256)(128)(2,1)S(1)} %pad_maximum_fusion.10), channel_id=1, source_target_pairs={{0,4},{1,5},{2,6},{3,7},{4,0},{5,1},{6,2},{7,3},{8,12},{9,13},{10,... | collective-permute-start | bytes 200 | tf_op jit(solution)/shard_map/ppermute | solution.py:15
  126.6 296.1 %copy-start.1 = (bf16[2,256,256]{2,1,0:T(8,128)(2,1)S(1)}, bf16[2,256,256]{2,1,0:T(8,128)(2,1)}, u32[]{:S(2)}) copy-start(bf16[2,256,256]{2,1,0:T(8,128)(2,1)} %param.15) | copy-start | bytes 786436
  400.3 12.3 %all-to-all-start = ((bf16[8,8,320]{2,1,0:T(8,128)(2,1)}), bf16[8,8,320]{2,1,0:T(8,128)(2,1)S(1)}, u32[]{:S(2)}, u32[]{:S(2)}) async-start(bf16[8,8,320]{2,1,0:T(8,128)(2,1)} %stack.2), calls=%async_computation | async-start | bytes 98304 | tf_op jit(solution)/shard_map/all_to_all | solution.py:40
  403.8 4.3 collective-permute-start.13
  412.8 18.2 %copy-start.24 = (f32[8]{0:T(128)S(1)}, f32[8]{0:T(128)}, u32[]{:S(2)}) copy-start(f32[8]{0:T(128)} %convert_element_type.88) | copy-start | bytes 100
  413.2 10.9 %collective-permute-start = (bf16[8,2,256]{2,0,1:T(8,128)(2,1)S(1)}, bf16[8,2,256]{2,0,1:T(8,128)(2,1)S(1)}, u32[]{:S(2)}, u32[]{:S(2)}) collective-permute-start(bf16[8,2,256]{2,0,1:T(8,128)(2,1)S(1)} %fusion.50), channel_id=1, source_target_pairs={{0,1},{1,0},{2,3},{3,2},{4,5},{5,4},{6,7},{7,6},{8,9},{9,8},{10,11... | collective-permute-start | bytes 24584 | tf_op jit(solution)/shard_map/ppermute | solution.py:15
  424.1 7.6 %collective-permute-start.4 = (bf16[16,2,256]{2,0,1:T(8,128)(2,1)S(1)}, bf16[16,2,256]{2,0,1:T(8,128)(2,1)S(1)}, u32[]{:S(2)}, u32[]{:S(2)}) collective-permute-start(bf16[16,2,256]{2,0,1:T(8,128)(2,1)S(1)} %pad_maximum_fusion.8), channel_id=1, source_target_pairs={{0,2},{1,3},{2,0},{3,1},{4,6},{5,7},{6,4},{7,5},{8,10},{9,11},{10,... | collective-permute-start | bytes 49160 | tf_op jit(solution)/shard_map/ppermute | solution.py:15
  426.1 0.7 copy-start.4
  427.6 16.3 %collective-permute-start.6 = (bf16[2,512,256]{1,2,0:T(8,128)(2,1)}, bf16[2,512,256]{1,2,0:T(8,128)(2,1)S(1)}, u32[]{:S(2)}, u32[]{:S(2)}) collective-permute-start(bf16[2,512,256]{1,2,0:T(8,128)(2,1)} %pad_maximum_fusion.4), channel_id=1, source_target_pairs={{0,2},{1,3},{2,0},{3,1},{4,6},{5,7},{6,4},{7,5},{8,10},{9,11},{10,... | collective-permute-start | bytes 1572872 | tf_op jit(solution)/shard_map/ppermute | solution.py:15
  431.8 2.5 copy-start.9
  432.4 18.3 %collective-permute-start.8 = (bf16[32,2,256]{2,0,1:T(8,128)(2,1)}, bf16[32,2,256]{2,0,1:T(8,128)(2,1)}, u32[]{:S(2)}, u32[]{:S(2)}) collective-permute-start(bf16[32,2,256]{2,0,1:T(8,128)(2,1)} %pad_maximum_fusion.7), channel_id=1, source_target_pairs={{0,4},{1,5},{2,6},{3,7},{4,0},{5,1},{6,2},{7,3},{8,12},{9,13},{10,... | collective-permute-start | bytes 98312 | tf_op jit(solution)/shard_map/ppermute | solution.py:15
  435.5 12.4 %copy-start.19 = (bf16[16,2,128]{2,1,0:T(2,128)(2,1)S(1)}, bf16[16,2,128]{2,1,0:T(2,128)(2,1)}, u32[]{:S(2)}) copy-start(bf16[16,2,128]{2,1,0:T(2,128)(2,1)} %reshape_squeeze.34) | copy-start | bytes 24580
  446.0 50.5 %collective-permute-start.10 = (bf16[2,1024,256]{1,2,0:T(8,128)(2,1)}, bf16[2,1024,256]{1,2,0:T(8,128)(2,1)}, u32[]{:S(2)}, u32[]{:S(2)}) collective-permute-start(bf16[2,1024,256]{1,2,0:T(8,128)(2,1)} %pad_maximum_fusion.2), channel_id=1, source_target_pairs={{0,4},{1,5},{2,6},{3,7},{4,0},{5,1},{6,2},{7,3},{8,12},{9,13},{10,... | collective-permute-start | bytes 3145736 | tf_op jit(solution)/shard_map/ppermute | solution.py:15
  452.1 12.4 %collective-permute-start.12 = (bf16[64,2,256]{2,0,1:T(8,128)(2,1)}, bf16[64,2,256]{2,0,1:T(8,128)(2,1)}, u32[]{:S(2)}, u32[]{:S(2)}) collective-permute-start(bf16[64,2,256]{2,0,1:T(8,128)(2,1)} %pad_maximum_fusion.6), channel_id=1, source_target_pairs={{0,8},{1,9},{2,10},{3,11},{4,12},{5,13},{6,14},{7,15},{8,0},{9,1},... | collective-permute-start | bytes 196616 | tf_op jit(solution)/shard_map/ppermute | solution.py:15
  462.0 42.3 %collective-permute-start.7 = (bf16[2,512,256]{1,2,0:T(8,128)(2,1)}, bf16[2,512,256]{1,2,0:T(8,128)(2,1)}, u32[]{:S(2)}, u32[]{:S(2)}) collective-permute-start(bf16[2,512,256]{1,2,0:T(8,128)(2,1)} %pad_maximum_fusion.5), channel_id=1, source_target_pairs={{0,2},{1,3},{2,0},{3,1},{4,6},{5,7},{6,4},{7,5},{8,10},{9,11},{10,... | collective-permute-start | bytes 1572872 | tf_op jit(solution)/shard_map/ppermute | solution.py:15
  467.2 34.2 %copy-start.10 = (bf16[64,2,128]{2,1,0:T(2,128)(2,1)S(1)}, bf16[64,2,128]{2,1,0:T(2,128)(2,1)}, u32[]{:S(2)}) copy-start(bf16[64,2,128]{2,1,0:T(2,128)(2,1)} %reshape_squeeze.38) | copy-start | bytes 98308
  467.2 34.2 %copy-start.23 = (f32[64]{0:T(128)S(1)}, f32[64]{0:T(128)}, u32[]{:S(2)}) copy-start(f32[64]{0:T(128)} %convert_element_type.97) | copy-start | bytes 772
  499.5 60.8 %collective-permute-start.14 = (bf16[2,2048,256]{1,2,0:T(8,128)(2,1)}, bf16[2,2048,256]{1,2,0:T(8,128)(2,1)}, u32[]{:S(2)}, u32[]{:S(2)}) collective-permute-start(bf16[2,2048,256]{1,2,0:T(8,128)(2,1)} %pad_maximum_fusion), channel_id=1, source_target_pairs={{0,8},{1,9},{2,10},{3,11},{4,12},{5,13},{6,14},{7,15},{8,0},{9,1},... | collective-permute-start | bytes 6291464 | tf_op jit(solution)/shard_map/ppermute | solution.py:15
  504.3 3.3 copy-start.5
  505.7 47.7 %collective-permute-start.11 = (bf16[2,1024,256]{1,2,0:T(8,128)(2,1)S(1)}, bf16[2,1024,256]{1,2,0:T(8,128)(2,1)S(1)}, u32[]{:S(2)}, u32[]{:S(2)}) collective-permute-start(bf16[2,1024,256]{1,2,0:T(8,128)(2,1)S(1)} %pad_maximum_fusion.3), channel_id=1, source_target_pairs={{0,4},{1,5},{2,6},{3,7},{4,0},{5,1},{6,2},{7,3},{8,12},{9,13},{10,... | collective-permute-start | bytes 3145736 | tf_op jit(solution)/shard_map/ppermute | solution.py:15
  507.6 0.9 copy-start.15
  507.6 0.9 copy-start.17
  507.7 0.9 copy-start.20
  507.7 0.9 copy-start.21
  507.7 1.2 copy-start.2
  508.0 1.0 copy-start.7
  554.8 48.6 %collective-permute-start.15 = (bf16[2,2048,256]{1,2,0:T(8,128)(2,1)S(1)}, bf16[2,2048,256]{1,2,0:T(8,128)(2,1)S(1)}, u32[]{:S(2)}, u32[]{:S(2)}) collective-permute-start(bf16[2,2048,256]{1,2,0:T(8,128)(2,1)S(1)} %pad_maximum_fusion.1), channel_id=1, source_target_pairs={{0,8},{1,9},{2,10},{3,11},{4,12},{5,13},{6,14},{7,15},{8,0},{9,1},... | collective-permute-start | bytes 6291464 | tf_op jit(solution)/shard_map/ppermute | solution.py:15
  560.3 3.0 copy-start.14
  560.3 3.0 copy-start.16
  560.3 3.0 copy-start.6
  560.4 3.1 copy-start.8
  563.6 1.8 copy-start.18
  603.4 0.8 copy-start.11
  604.1 0.9 copy-start.22
Sparse Core Ops, SparseCore 0:
  20.0 104.5 all-reduce.2
